TPU v7x, 256 devices: a whole 4x4x8 slice. The times are simulated.
256 devices in a mesh: grp: 8 (over z), tp: 32 (over x, y, core).
Axes of the slice: x: 4, y: 4, z: 8, core: 2. Of those that a mesh axis runs over, the one named last changes fastest.
Arguments:
- hidden_in: bfloat16 [1024, 3584], P(('grp', 'tp')), may hold values from -6 to 6
- norm_gains: float32 [4, 3584], replicated, may hold values from 0.25 to 1.75
- w_qkv: bfloat16 [3584, 8192], P(None, 'tp'), may hold values from -0.09375 to 0.09375
- w_out: bfloat16 [4096, 3584], P('tp'), may hold values from -0.09375 to 0.09375
- w_gate_up: bfloat16 [2, 3584, 8192], P(None, None, 'tp'), may hold values from -0.09375 to 0.09375
- w_down: bfloat16 [8192, 3584], P('tp'), may hold values from -0.0625 to 0.0625
- prompt_keys: bfloat16 [32768, 2048], P(('grp', 'tp')), may hold values from -480 to 480, as said below
- prompt_values: bfloat16 [32768, 2048], P(('grp', 'tp')), may hold values from -6 to 6
- tail_keys: bfloat16 [1024, 64, 2048], P(('grp', 'tp')), may hold values from -480 to 480, as said below
- tail_values: bfloat16 [1024, 64, 2048], P(('grp', 'tp')), may hold values from -6 to 6
- prompt_len: int32 [80], replicated, may hold values from 1 to 4087, as said below
- group_home: int32 [80], replicated, may hold values from 0 to 7, as said below
- req_group: int32 [1024], P('grp'), may hold values from 0 to 79, as said below
- tail_len: int32 [1024], P('grp'), may hold values from 1 to 64, 32768 in all
Outputs:
- layer_out: bfloat16 [1024, 3584], P(('grp', 'tp'))
Inputs may be any that keep to these rules, and one draw needn't show every extreme that they name: `group_home`: each grp device is home to exactly 10 groups. `prompt_len`: the prompts of the groups homed on one grp device lie one after another in order of group id from the first of that device's 4096 cache positions; together they hold at most 4096 positions, exactly 4096 on one home in every draw, where one group holds 4087 of them. `req_group`: of the 128 requests held by one grp device, at most 32 belong to groups homed on any one grp device; in every draw one home receives exactly 32 requests from every grp device. `prompt_keys`: cached keys, already rotated. `tail_keys`: cached keys, already rotated.
All inputs are finite; a program needn't handle non-finite values. No bound on the sum of `tail_len` on one device may be relied on, other than what follows from the above.
Results may differ from a plain program's by a relative error of at most 0.015.
Values may be sent and summed in bfloat16 or wider, within the bound.
A program may use at most 128 MiB of HBM per device.

v0:
```python
import math
import jax
import jax.numpy as jnp
from jax import lax
from jax.sharding import PartitionSpec as P

HEADS = 16
KV_HEADS = 8
HEAD_DIM = 256
NORM_EPS = 1e-06
SOFT_CAP = 50.0


def rms_scale(values, gain_row):
    values = values.astype(jnp.float32)
    return (
        values * lax.rsqrt(jnp.mean(values * values, axis=-1, keepdims=True) + NORM_EPS) * gain_row
    )


def rotate(head_rows, position):
    half_width = head_rows.shape[-1] // 2
    freq_index = jnp.arange(half_width).astype(jnp.float32)
    frequency = jnp.exp(freq_index * (-math.log(10000.0) / half_width))
    angles = position.astype(jnp.float32)[:, None] * frequency[None, :]
    cosine = jnp.cos(angles)[:, None, :]
    sine_part = jnp.sin(angles)[:, None, :]
    head_rows = head_rows.astype(jnp.float32)
    first_half = head_rows[..., :half_width]
    second = head_rows[..., half_width:]
    return jnp.concatenate(
        [first_half * cosine - second * sine_part, second * cosine + first_half * sine_part],
        axis=-1,
    )


def capped(scores):
    return SOFT_CAP * jnp.tanh(scores * HEAD_DIM ** (-0.5) / SOFT_CAP)


def lookup(lookup_table, index_list):
    matches = index_list[:, None] == jnp.arange(lookup_table.shape[0], dtype=jnp.int32)[None, :]
    return jnp.sum(jnp.where(matches, lookup_table[None, :], 0), axis=1)


def group_starts(prompt_len, group_home):
    group_ids = jnp.arange(prompt_len.shape[0], dtype=jnp.int32)
    same_home = group_home[:, None] == group_home[None, :]
    earlier = group_ids[None, :] < group_ids[:, None]
    return jnp.sum(jnp.where(same_home & earlier, prompt_len[None, :], 0), axis=1)


def shared_part(queries, key_rows, value_rows, visible):
    scores = capped(
        jnp.einsum("nkjd,pkd->nkjp", queries, key_rows, preferred_element_type=jnp.float32)
    )
    exponent = jnp.where(visible[:, None, None, :], jnp.exp(scores), 0.0)
    numerator = jnp.einsum(
        "nkjp,pkd->nkjd",
        exponent.astype(jnp.bfloat16),
        value_rows,
        preferred_element_type=jnp.float32,
    )
    return (numerator, jnp.sum(exponent, axis=-1))


def own_part(queries, key_rows, value_rows, visible):
    scores = capped(
        jnp.einsum("nkjd,npkd->nkjp", queries, key_rows, preferred_element_type=jnp.float32)
    )
    exponent = jnp.where(visible[:, None, None, :], jnp.exp(scores), 0.0)
    numerator = jnp.einsum(
        "nkjp,npkd->nkjd",
        exponent.astype(jnp.bfloat16),
        value_rows,
        preferred_element_type=jnp.float32,
    )
    return (numerator, jnp.sum(exponent, axis=-1))


def per_device(
    hidden_in,
    norm_gains,
    w_qkv,
    w_out,
    w_gate_up,
    w_down,
    prompt_keys,
    prompt_values,
    tail_keys,
    tail_values,
    prompt_len,
    group_home,
    req_group,
    tail_len,
):
    tp_rank = lax.axis_index("tp")
    q_width = HEADS * HEAD_DIM
    kv_width = KV_HEADS * HEAD_DIM
    row_count = hidden_in.shape[0]
    normed = rms_scale(hidden_in, norm_gains[0]).astype(jnp.bfloat16)
    qkv_share = jnp.dot(
        lax.all_gather(normed, "tp", axis=0, tiled=True), w_qkv, preferred_element_type=jnp.float32
    ).astype(jnp.bfloat16)
    projected_qkv = lax.all_gather(qkv_share, "tp", axis=1, tiled=True)
    requests = projected_qkv.shape[0]
    req_len = lookup(prompt_len, req_group)
    position = req_len + tail_len
    queries = rotate(
        projected_qkv[:, :q_width].reshape(requests, HEADS, HEAD_DIM), position
    ).astype(jnp.bfloat16)
    queries = queries.reshape(requests, KV_HEADS, 2, HEAD_DIM)
    key_new = rotate(
        projected_qkv[:, q_width : q_width + kv_width].reshape(requests, KV_HEADS, HEAD_DIM),
        position,
    ).astype(jnp.bfloat16)
    value_new = projected_qkv[:, q_width + kv_width :].reshape(requests, KV_HEADS, HEAD_DIM)
    starts = group_starts(prompt_len, group_home)
    req_home = lookup(group_home, req_group)
    req_start = lookup(starts, req_group)
    cap_dev = prompt_keys.shape[0]
    row_first = tp_rank * row_count
    own_queries = lax.dynamic_slice_in_dim(queries, row_first, row_count, 0)
    own_tail_len = lax.dynamic_slice_in_dim(tail_len, row_first, row_count, 0)
    tail_dev = tail_keys.shape[1]
    tail_pos = jnp.arange(tail_dev, dtype=jnp.int32)
    own_num, own_den = own_part(
        own_queries,
        tail_keys.reshape(row_count, tail_dev, KV_HEADS, HEAD_DIM),
        tail_values.reshape(row_count, tail_dev, KV_HEADS, HEAD_DIM),
        tail_pos[None, :] < own_tail_len[:, None],
    )
    numerator = lax.dynamic_update_slice_in_dim(
        jnp.zeros((requests, KV_HEADS, 2, HEAD_DIM), jnp.float32), own_num, row_first, 0
    )
    denominator = lax.dynamic_update_slice_in_dim(
        jnp.zeros((requests, KV_HEADS, 2), jnp.float32), own_den, row_first, 0
    )
    key_piece = lax.all_gather(prompt_keys, "grp", axis=0, tiled=True)
    value_piece = lax.all_gather(prompt_values, "grp", axis=0, tiled=True)
    piece_rows = key_piece.shape[0]
    gathered_index = jnp.arange(piece_rows, dtype=jnp.int32)
    home_index = gathered_index // cap_dev
    piece_offsets = tp_rank * cap_dev + gathered_index % cap_dev
    visible = (
        (home_index[None, :] == req_home[:, None])
        & (piece_offsets[None, :] >= req_start[:, None])
        & (piece_offsets[None, :] < (req_start + req_len)[:, None])
    )
    part_num, part_den = shared_part(
        queries,
        key_piece.reshape(piece_rows, KV_HEADS, HEAD_DIM),
        value_piece.reshape(piece_rows, KV_HEADS, HEAD_DIM),
        visible,
    )
    numerator, denominator = (numerator + part_num, denominator + part_den)
    share_width = w_out.shape[0]
    first_col = tp_rank * share_width
    flat_num = numerator.reshape(requests, q_width)
    flat_den = denominator.reshape(requests, HEADS)
    total_num, total_den = lax.psum((flat_num, flat_den), "tp")
    share_num = lax.dynamic_slice_in_dim(total_num, first_col, share_width, 1)
    self_exp = jnp.exp(
        capped(jnp.einsum("nkjd,nkd->nkj", queries, key_new, preferred_element_type=jnp.float32))
    )
    self_num = (
        lax.optimization_barrier(self_exp.astype(jnp.bfloat16)).astype(jnp.float32)[..., None]
        * value_new.astype(jnp.float32)[:, :, None, :]
    )
    self_share = lax.dynamic_slice_in_dim(
        self_num.reshape(requests, q_width), first_col, share_width, 1
    )
    total_den = total_den + self_exp.reshape(requests, HEADS)
    head_of_col = (first_col + jnp.arange(share_width, dtype=jnp.int32)) // HEAD_DIM
    head_pick = (head_of_col[None, :] == jnp.arange(HEADS, dtype=jnp.int32)[:, None]).astype(
        jnp.float32
    )
    den_cols = jnp.dot(total_den, head_pick, precision=lax.Precision.HIGHEST)
    attn_share = ((share_num + self_share) / den_cols).astype(jnp.bfloat16)
    block_rows = attn_share
    attn_proj = lax.psum_scatter(
        jnp.dot(block_rows, w_out, preferred_element_type=jnp.float32),
        "tp",
        scatter_dimension=0,
        tiled=True,
    )
    resid = (hidden_in.astype(jnp.float32) + rms_scale(attn_proj, norm_gains[1])).astype(
        jnp.bfloat16
    )
    ffn_in = rms_scale(resid, norm_gains[2]).astype(jnp.bfloat16)
    gate_up = jnp.einsum(
        "rd,kdf->krf",
        lax.all_gather(ffn_in, "tp", axis=0, tiled=True),
        w_gate_up,
        preferred_element_type=jnp.float32,
    )
    hidden_units = (jax.nn.gelu(gate_up[0], approximate=True) * gate_up[1]).astype(jnp.bfloat16)
    block_rows = hidden_units
    ffn_proj = lax.psum_scatter(
        jnp.dot(block_rows, w_down, preferred_element_type=jnp.float32).astype(jnp.bfloat16),
        "tp",
        scatter_dimension=0,
        tiled=True,
    ).astype(jnp.float32)
    return (resid.astype(jnp.float32) + rms_scale(ffn_proj, norm_gains[3])).astype(jnp.bfloat16)


def solution(mesh):
    in_specs = (
        P(("grp", "tp"), None),
        P(),
        P(None, "tp"),
        P("tp", None),
        P(None, None, "tp"),
        P("tp", None),
        P(("grp", "tp"), None),
        P(("grp", "tp"), None),
        P(("grp", "tp"), None, None),
        P(("grp", "tp"), None, None),
        P(),
        P(),
        P("grp"),
        P("grp"),
    )
    out_specs = P(("grp", "tp"), None)
    return jax.shard_map(
        per_device, mesh=mesh, in_specs=in_specs, out_specs=out_specs, check_vma=False
    )
```

profile of v0, /device:TPU:1, one launch (start us, length us, event | category | flops | bytes accessed | tf_op | source)
XLA Modules:
  0.0 625.6 jit_solution(4266515688802575155)
XLA Ops:
  6.5 1.2 slice_reduce_fusion.1
  7.7 0.9 fusion.35
  8.6 0.8 fusion.47
  9.5 26.6 %all-gather = bf16[32,4,3584]{2,1,0:T(4,128)(2,1)S(1)} all-gather(bf16[1,4,3584]{2,1,0:T(4,128)(2,1)S(1)} %fusion.47), channel_id=1, replica_groups=mesh['grp'=8,'tp'=32] {'tp'}, dimensions={0}, use_global_device_ids=true | all-gather | bytes 946176 | tf_op jit(solution)/shard_map/all_gather | solution.py:103
  36.0 1.1 reshape.279
  37.2 2.9 convolution_convert_fusion.1
  40.1 1.0 copy.77
  41.2 1.0 copy.79
  42.3 0.0 all-reduce.6.cloned.1.call-start
  42.3 0.1 dynamic_slice.12
  42.5 0.2 select_reduce_fusion.2
  42.6 0.1 select_reduce_fusion.3
  42.8 0.1 iota_compare_fusion.4
  42.8 0.3 multiply_cosine_fusion
  43.1 0.9 compare_and_fusion
  44.0 46.5 %all-gather.6.cloned.1.call-done = bf16[128,8192]{1,0:T(8,128)(2,1)} async-done(((bf16[128,256]{1,0:T(8,128)(2,1)}), bf16[128,8192]{1,0:T(8,128)(2,1)}) %all-gather.6.cloned.1.call-update) | async-done | bytes 2097168 | tf_op jit(solution)/shard_map/all_gather | solution.py:105
  90.5 1.4 slice_convert_fusion
  91.9 0.7 copy.101
  92.6 0.3 subtract_convert_fusion
  92.9 0.1 copy.75
  93.1 0.1 copy.76
  93.2 0.9 copy-done.11
  94.1 0.5 fusion.73
  94.6 0.1 copy.88
  94.7 2.4 slice_convert_fusion.2
  97.2 0.3 copy.102
  97.5 0.1 subtract_convert_fusion.1
  97.7 0.1 maximum_bitcast_fusion
  97.8 1.2 pad_maximum_fusion
  98.9 0.3 fusion.10
  99.2 50.9 %all-gather.8.cloned.1.call-done = bf16[1024,2048]{0,1:T(8,128)(2,1)} async-done(((bf16[128,2048]{0,1:T(8,128)(2,1)}), bf16[1024,2048]{0,1:T(8,128)(2,1)}) %all-gather.8.cloned.1.call-update) | async-done | bytes 4194320 | tf_op jit(solution)/shard_map/all_gather | solution.py:139
  150.1 7.7 %bitcast_reduce_fusion = (f32[128,8,2]{0,2,1:T(2,128)S(1)}, f32[8,128,2,1024]{3,1,2,0:T(8,128)}) fusion(pred[128,1024]{1,0:T(8,128)(4,1)} %compare_and_fusion, bf16[1024,8,256,1]{0,2,3,1:T(8,128)(2,1)} %bitcast.96, bf16[128,8,2,128]{3,0,2,1:T(8,128)(2,1)S(1)} %bitcast.87, bf16[128,8,2,128]{3,0,2,1:T(8,128)(2,1)S(1)} %bitcast.84), kind=kOutput, calls=%fused_computation | convolution fusion | flops 1084225536 | bytes 13770752 | tf_op jit(solution)/shard_map/nkjd,pkd->nkjp/dot_general | solution.py:55
  157.8 55.1 %all-gather.10.cloned.1.call-done = bf16[1024,2048]{0,1:T(8,128)(2,1)} async-done(((bf16[128,2048]{0,1:T(8,128)(2,1)}), bf16[1024,2048]{0,1:T(8,128)(2,1)}) %all-gather.10.cloned.1.call-update) | async-done | bytes 4194320 | tf_op jit(solution)/shard_map/all_gather | solution.py:140
  212.9 7.0 %fusion = f32[8,128,2,256]{3,1,2,0:T(8,128)S(1)} fusion(bf16[1024,8,256,1]{0,2,3,1:T(8,128)(2,1)} %bitcast.97, f32[8,128,2,1024]{3,1,2,0:T(8,128)} %get-tuple-element.27, pred[128,1024]{1,0:T(8,128)(4,1)} %compare_and_fusion), kind=kOutput, calls=%fused_computation.4 | convolution fusion | flops 1082130432 | bytes 14811136 | tf_op jit(solution)/shard_map/nkjp,pkd->nkjd/dot_general | solution.py:58
  220.0 1.4 copy.123
  221.3 0.7 fusion.28
  222.0 2.9 copy.85
  224.9 2.9 copy.86
  227.8 0.2 all-reduce.8.cloned.1.call-start
  228.1 3.4 fusion.15
  231.4 1.2 copy.94
  232.7 0.2 copy.87
  232.9 0.3 copy.103
  233.3 2.8 broadcast_multiply_fusion
  236.1 4.0 mul.269
  240.1 0.1 dynamic-slice_add_fusion
  240.2 1.3 add.147
  241.4 67.5 %psum.15 = f32[128,16]{0,1:T(8,128)S(1)} all-reduce(f32[128,16]{0,1:T(8,128)S(1)} %bitcast.94), channel_id=1, replica_groups=mesh['grp'=8,'tp'=32] {'tp'}, use_global_device_ids=true, to_apply=%region_8.9 | all-reduce | flops 2048 | bytes 16384 | tf_op jit(solution)/shard_map/psum | solution.py:161
  309.0 38.9 %all-reduce.6.cloned.1.call-done = f32[128,4096]{1,0:T(8,128)} async-done(((f32[128,4096]{1,0:T(8,128)}), f32[128,4096]{1,0:T(8,128)}) %all-reduce.6.cloned.1.call-update) | async-done | bytes 2097168 | tf_op jit(solution)/shard_map/psum | solution.py:161
  347.9 1.1 fusion.5
  349.1 1.6 fusion.74
  350.7 0.0 all-reduce.10.cloned.1.call-start
  350.8 0.6 dynamic-slice.6
  352.0 115.3 %all-reduce.8.cloned.1.call-done = f32[128,3584]{1,0:T(8,128)} async-done(((f32[128,3584]{1,0:T(8,128)}), f32[128,3584]{1,0:T(8,128)}) %all-reduce.8.cloned.1.call-update) | async-done | bytes 1835024
  467.4 1.0 multiply_reduce_fusion
  468.4 1.1 fusion.39
  469.5 0.1 fusion.46
  469.6 28.2 %all-gather.1 = bf16[32,4,3584]{2,1,0:T(4,128)(2,1)} all-gather(bf16[1,4,3584]{2,1,0:T(4,128)(2,1)S(1)} %fusion.46), channel_id=1, replica_groups=mesh['grp'=8,'tp'=32] {'tp'}, dimensions={0}, use_global_device_ids=true | all-gather | bytes 946176 | tf_op jit(solution)/shard_map/all_gather | solution.py:193
  497.9 1.7 reshape.286
  499.5 2.7 convolution_bitcast_fusion
  502.2 1.4 convolution_convert_fusion
  503.7 112.7 %all-reduce.10.cloned.1.call-done = bf16[128,3584]{1,0:T(8,128)(2,1)} async-done(((bf16[128,3584]{1,0:T(8,128)(2,1)}), bf16[128,3584]{1,0:T(8,128)(2,1)}) %all-reduce.10.cloned.1.call-update) | async-done | bytes 917520
  616.3 1.0 fusion.33
  617.3 1.5 fusion.42
  (45 shorter events, 0.4 us)
Async XLA Ops:
  6.5 495.7 %copy-start = (bf16[256,3584]{1,0:T(8,128)(2,1)S(1)}, bf16[256,3584]{1,0:T(8,128)(2,1)}, u32[]{:S(2)}) copy-start(bf16[256,3584]{1,0:T(8,128)(2,1)} %param.19) | copy-start | bytes 5505028
  6.5 83.9 %all-gather.6.cloned.1.call-start = ((), (), s32[]{:S(2)}) async-start(), calls=%async_computation | async-start | bytes 2162688 | tf_op jit(solution)/shard_map/all_gather | solution.py:105
  36.0 4.1 copy-start.4
  37.2 4.0 copy-start.5
  40.0 2.3 copy-start.10
  40.1 2.4 copy-start.7
  40.1 2.4 copy-start.8
  40.1 2.6 copy-start.9
  40.1 110.0 %all-gather.8.cloned.1.call-start = ((), (), s32[]{:S(2)}) async-start(), calls=%async_computation.1 | async-start | bytes 4718592 | tf_op jit(solution)/shard_map/all_gather | solution.py:139
  41.2 171.8 %all-gather.10.cloned.1.call-start = ((), (), s32[]{:S(2)}) async-start(), calls=%async_computation.2 | async-start | bytes 4718592 | tf_op jit(solution)/shard_map/all_gather | solution.py:140
  42.3 305.7 %all-reduce.6.cloned.1.call-start = ((), (), s32[]{:S(2)}) async-start(), calls=%async_computation.3 | async-start | bytes 4194304 | tf_op jit(solution)/shard_map/psum | solution.py:161
  92.9 1.2 copy-start.11
  97.5 1.4 copy-start.2
  227.8 5.1 copy-start.1
  227.8 239.5 %all-reduce.8.cloned.1.call-start = ((), (), s32[]{:S(2)}) async-start(), calls=%async_computation.4 | async-start | bytes 3670016
  236.1 113.0 %copy-start.3 = (bf16[128,3584]{1,0:T(8,128)(2,1)S(1)}, bf16[128,3584]{1,0:T(8,128)(2,1)}, u32[]{:S(2)}) copy-start(bf16[128,3584]{1,0:T(8,128)(2,1)} %param.17) | copy-start | bytes 2752516
  349.1 1.7 copy-start.12
  349.1 119.3 %copy-start.6 = (bf16[4,3584]{1,0:T(4,128)(2,1)S(1)}, bf16[4,3584]{1,0:T(4,128)(2,1)}, u32[]{:S(2)}) copy-start(bf16[4,3584]{1,0:T(4,128)(2,1)} %param.14) | copy-start | bytes 86020
  350.7 265.6 %all-reduce.10.cloned.1.call-start = ((), (), s32[]{:S(2)}) async-start(), calls=%async_computation.5 | async-start | bytes 1835008
Sparse Core Ops, SparseCore 0:
  40.2 50.2 all-gather.5
  92.2 57.8 all-gather.7
  151.8 61.1 all-gather.9
  228.0 119.9 all-reduce.5
  351.1 116.2 all-reduce.7
  503.8 112.4 all-reduce.9
where the time goes:
time: 626 us
  waiting for transfers between devices  419 us (67%)
  blocking collectives  122 us (19%)
  matrix products  28.5 us (5%)
  local copies, waits for them, and re-layouts  23.3 us (4%)
  other arithmetic  17.2 us (3%)
  between operations  14.4 us (2%)
    unnamed x8, waiting for transfers between devices  228 us
    psum x1, blocking collectives, per_device(): total_num, total_den = lax.psum((flat_num, flat_den), 'tp')  67.5 us
    all_gather x1, waiting for transfers between devices, per_device(): value_piece = lax.all_gather(prompt_values, 'grp', axis=0, tiled=True)  55.1 us
    all_gather x1, waiting for transfers between devices, per_device(): key_piece = lax.all_gather(prompt_keys, 'grp', axis=0, tiled=True)  50.9 us
    all_gather x1, waiting for transfers between devices, per_device(): projected_qkv = lax.all_gather(qkv_share, 'tp', axis=1, tiled=True)  46.5 us
    psum x1, waiting for transfers between devices, per_device(): total_num, total_den = lax.psum((flat_num, flat_den), 'tp')  38.9 us
    all_gather x1, blocking collectives, per_device(): lax.all_gather(ffn_in, 'tp', axis=0, tiled=True)  28.2 us
    all_gather x1, blocking collectives, per_device(): lax.all_gather(normed, 'tp', axis=0, tiled=True)  26.6 us
  transfers between devices with their start and end apart: 6, of which 6 were waited for; matrix products, arithmetic and copies ran while one was open for 5% of the time, Pallas kernels for 0%

commit v1 on v0

--- a/solution.py
+++ b/solution.py
@@ -136,7 +136,8 @@
     denominator = lax.dynamic_update_slice_in_dim(
         jnp.zeros((requests, KV_HEADS, 2), jnp.float32), own_den, row_first, 0
     )
-    key_piece = lax.all_gather(prompt_keys, "grp", axis=0, tiled=True)
+    copies = jnp.concatenate([prompt_keys] * lax.axis_size("grp"), axis=0)
+    key_piece = lax.all_to_all(copies, "grp", 0, 0, tiled=True)
     value_piece = lax.all_gather(prompt_values, "grp", axis=0, tiled=True)
     piece_rows = key_piece.shape[0]
     gathered_index = jnp.arange(piece_rows, dtype=jnp.int32)

time: 626 us -> 598 us (0.955)
  waiting for transfers between devices: 419 us -> 383 us
  starting transfers between devices: 0.39 us -> 8.89 us
    all_to_all x0 -> x1, waiting for transfers between devices: none -> 62.2 us  [per_device(): key_piece = lax.all_to_all(copies, 'grp', 0, 0, tiled=True)]
    all_gather x1 -> x0, waiting for transfers between devices: 50.9 us -> none  [per_device(): key_piece = lax.all_gather(prompt_keys, 'grp', axis=0, tiled=True)]
    all_gather x1, waiting for transfers between devices: 55.1 us -> 18.5 us  [per_device(): value_piece = lax.all_gather(prompt_values, 'grp', axis=0, tiled=True)]
    all_gather x1, waiting for transfers between devices: 46.5 us -> 36.5 us  [per_device(): projected_qkv = lax.all_gather(qkv_share, 'tp', axis=1, tiled=True)]
    all_to_all x0 -> x1, starting transfers between devices: none -> 8.33 us  [per_device(): key_piece = lax.all_to_all(copies, 'grp', 0, 0, tiled=True)]
    unnamed x35 -> x46, local copies, waits for them, and re-layouts: 9.03 us -> 13.7 us
    unnamed x8 -> x7, waiting for transfers between devices: 228 us -> 228 us
  transfers between devices with their start and end apart: 6 -> 6, of which waited for: 6 -> 6; matrix products, arithmetic and copies ran while one was open for 5% -> 6% of each run, Pallas kernels for 0% -> 0%
where the time goes in v1:
time: 598 us; the launch traced here: 597 us
  waiting for transfers between devices  383 us (64%)
  blocking collectives  119 us (20%)
  local copies, waits for them, and re-layouts  28 us (5%)
  matrix products  26 us (4%)
  other arithmetic  17.3 us (3%)
  between operations  14.2 us (2%)
  starting transfers between devices  8.89 us (1%)
    unnamed x7, waiting for transfers between devices  228 us
    psum x1, blocking collectives, per_device(): total_num, total_den = lax.psum((flat_num, flat_den), 'tp')  64.7 us
    all_to_all x1, waiting for transfers between devices, per_device(): key_piece = lax.all_to_all(copies, 'grp', 0, 0, tiled=True)  62.2 us
    psum x1, waiting for transfers between devices, per_device(): total_num, total_den = lax.psum((flat_num, flat_den), 'tp')  37.9 us
    all_gather x1, waiting for transfers between devices, per_device(): projected_qkv = lax.all_gather(qkv_share, 'tp', axis=1, tiled=True)  36.5 us
    all_gather x1, blocking collectives, per_device(): lax.all_gather(ffn_in, 'tp', axis=0, tiled=True)  28.2 us
    all_gather x1, blocking collectives, per_device(): lax.all_gather(normed, 'tp', axis=0, tiled=True)  26.6 us
    all_gather x1, waiting for transfers between devices, per_device(): value_piece = lax.all_gather(prompt_values, 'grp', axis=0, tiled=True)  18.5 us
  transfers between devices with their start and end apart: 6, of which 6 were waited for; matrix products, arithmetic and copies ran while one was open for 6% of the time, Pallas kernels for 0%

profile of v1, /device:TPU:1, one launch (start us, length us, event | category | flops | bytes accessed | tf_op | source)
XLA Modules:
  0.0 597.0 jit_solution(4218699757436684468)
XLA Ops:
  6.5 1.2 slice_reduce_fusion.1
  7.8 0.9 fusion.40
  8.7 0.8 fusion.52
  9.5 26.6 %all-gather = bf16[32,4,3584]{2,1,0:T(4,128)(2,1)S(1)} all-gather(bf16[1,4,3584]{2,1,0:T(4,128)(2,1)S(1)} %fusion.52), channel_id=1, replica_groups=mesh['grp'=8,'tp'=32] {'tp'}, dimensions={0}, use_global_device_ids=true | all-gather | bytes 946176 | tf_op jit(solution)/shard_map/all_gather | solution.py:103
  36.1 1.1 reshape.282
  37.2 2.8 convolution_convert_fusion.1
  40.5 2.0 copy-done.2
  42.4 8.3 %all-to-all-start = ((bf16[8,128,2048]{2,1,0:T(8,128)(2,1)}), bf16[8,128,2048]{2,1,0:T(8,128)(2,1)}, u32[]{:S(2)}, u32[]{:S(2)}) async-start(bf16[8,128,2048]{2,1,0:T(8,128)(2,1)} %bitcast.85), calls=%async_computation | async-start | bytes 8388608 | tf_op jit(solution)/shard_map/all_to_all | solution.py:140
  50.8 1.0 copy.79
  51.8 0.2 all-reduce.6.cloned.1.call-start
  52.1 0.1 dynamic_slice.12
  52.2 0.2 select_reduce_fusion.2
  52.4 0.1 select_reduce_fusion.3
  52.5 0.1 iota_compare_fusion.4
  52.6 0.3 multiply_cosine_fusion
  52.9 1.0 compare_and_fusion
  53.9 36.5 %all-gather.5.cloned.1.call-done = bf16[128,8192]{1,0:T(8,128)(2,1)} async-done(((bf16[128,256]{1,0:T(8,128)(2,1)}), bf16[128,8192]{1,0:T(8,128)(2,1)}) %all-gather.5.cloned.1.call-update) | async-done | bytes 2097168 | tf_op jit(solution)/shard_map/all_gather | solution.py:105
  90.4 1.4 slice_convert_fusion
  91.9 0.7 copy.104
  92.5 0.3 subtract_convert_fusion
  92.9 0.1 copy.76
  93.0 0.1 copy.77
  93.2 0.6 copy-done.13
  93.8 0.5 fusion.77
  94.2 0.1 copy.89
  94.4 2.4 slice_convert_fusion.2
  96.8 0.3 copy.105
  97.1 0.1 subtract_convert_fusion.1
  97.4 1.2 pad_maximum_fusion
  98.6 0.3 fusion.15
  98.8 62.2 %all-to-all-done = bf16[8,128,2048]{2,1,0:T(8,128)(2,1)} async-done(((bf16[8,128,2048]{2,1,0:T(8,128)(2,1)}), bf16[8,128,2048]{2,1,0:T(8,128)(2,1)}, u32[]{:S(2)}, u32[]{:S(2)}) %all-to-all-start) | async-done | bytes 4194336 | tf_op jit(solution)/shard_map/all_to_all | solution.py:140
  161.0 3.8 copy.103
  164.7 5.1 fusion
  169.9 18.5 %all-gather.7.cloned.1.call-done = bf16[1024,2048]{0,1:T(8,128)(2,1)} async-done(((bf16[128,2048]{0,1:T(8,128)(2,1)}), bf16[1024,2048]{0,1:T(8,128)(2,1)}) %all-gather.7.cloned.1.call-update) | async-done | bytes 4194320 | tf_op jit(solution)/shard_map/all_gather | solution.py:141
  188.3 7.2 %fusion.2 = f32[8,128,2,256]{3,1,2,0:T(8,128)S(1)} fusion(bf16[1024,8,256,1]{0,2,3,1:T(8,128)(2,1)} %bitcast.101, f32[8,1024,128,2]{2,1,3,0:T(8,128)} %get-tuple-element.27, pred[128,1024]{0,1:T(8,128)(4,1)} %compare_and_fusion), kind=kOutput, calls=%fused_computation.4 | convolution fusion | flops 1082130432 | bytes 14811136 | tf_op jit(solution)/shard_map/nkjp,pkd->nkjd/dot_general | solution.py:58
  195.5 1.4 copy.137
  196.9 0.7 fusion.33
  197.6 2.9 copy.86
  200.5 2.9 copy.87
  203.4 0.3 all-reduce.8.cloned.1.call-start
  203.7 3.3 fusion.20
  207.0 1.2 copy.96
  208.3 0.2 copy.88
  208.5 0.3 copy.106
  208.9 2.8 broadcast_multiply_fusion
  211.7 4.0 mul.269
  215.6 0.1 dynamic-slice_add_fusion
  215.7 1.3 add.147
  217.0 64.7 %psum.15 = f32[128,16]{0,1:T(8,128)S(1)} all-reduce(f32[128,16]{0,1:T(8,128)S(1)} %bitcast.99), channel_id=1, replica_groups=mesh['grp'=8,'tp'=32] {'tp'}, use_global_device_ids=true, to_apply=%region_8.9 | all-reduce | flops 2048 | bytes 16384 | tf_op jit(solution)/shard_map/psum | solution.py:162
  281.7 37.9 %all-reduce.6.cloned.1.call-done = f32[128,4096]{1,0:T(8,128)} async-done(((f32[128,4096]{1,0:T(8,128)}), f32[128,4096]{1,0:T(8,128)}) %all-reduce.6.cloned.1.call-update) | async-done | bytes 2097168 | tf_op jit(solution)/shard_map/psum | solution.py:162
  319.5 1.1 fusion.10
  320.7 1.6 fusion.78
  322.4 0.6 dynamic-slice.6
  323.6 115.3 %all-reduce.8.cloned.1.call-done = f32[128,3584]{1,0:T(8,128)} async-done(((f32[128,3584]{1,0:T(8,128)}), f32[128,3584]{1,0:T(8,128)}) %all-reduce.8.cloned.1.call-update) | async-done | bytes 1835024
  439.0 1.0 multiply_reduce_fusion
  440.0 1.1 fusion.44
  441.1 0.1 fusion.51
  441.2 28.2 %all-gather.1 = bf16[32,4,3584]{2,1,0:T(4,128)(2,1)} all-gather(bf16[1,4,3584]{2,1,0:T(4,128)(2,1)S(1)} %fusion.51), channel_id=1, replica_groups=mesh['grp'=8,'tp'=32] {'tp'}, dimensions={0}, use_global_device_ids=true | all-gather | bytes 946176 | tf_op jit(solution)/shard_map/all_gather | solution.py:194
  469.5 1.7 reshape.289
  471.1 2.7 convolution_bitcast_fusion
  473.8 1.4 convolution_convert_fusion
  475.3 112.7 %all-reduce.10.cloned.1.call-done = bf16[128,3584]{1,0:T(8,128)(2,1)} async-done(((bf16[128,3584]{1,0:T(8,128)(2,1)}), bf16[128,3584]{1,0:T(8,128)(2,1)}) %all-reduce.10.cloned.1.call-update) | async-done | bytes 917520
  588.0 1.0 fusion.38
  589.0 1.5 fusion.47
  (56 shorter events, 0.7 us)
Async XLA Ops:
  6.5 467.3 %copy-start = (bf16[256,3584]{1,0:T(8,128)(2,1)S(1)}, bf16[256,3584]{1,0:T(8,128)(2,1)}, u32[]{:S(2)}) copy-start(bf16[256,3584]{1,0:T(8,128)(2,1)} %param.19) | copy-start | bytes 5505028
  6.5 33.5 %copy-start.1 = (bf16[128,2048]{1,0:T(8,128)(2,1)S(1)}, bf16[128,2048]{1,0:T(8,128)(2,1)}, u32[]{:S(2)}) copy-start(bf16[128,2048]{1,0:T(8,128)(2,1)} %param.20) | copy-start | bytes 1572868
  6.5 83.9 %all-gather.5.cloned.1.call-start = ((), (), s32[]{:S(2)}) async-start(), calls=%async_computation.1 | async-start | bytes 2162688 | tf_op jit(solution)/shard_map/all_gather | solution.py:105
  40.4 2.0 copy-start.2
  42.4 8.4 %copy-start.6 = (bf16[128,2048]{1,0:T(8,128)(2,1)S(1)}, bf16[128,2048]{1,0:T(8,128)(2,1)}, u32[]{:S(2)}) copy-start(bf16[128,2048]{1,0:T(8,128)(2,1)} %param.21) | copy-start | bytes 1572868
  42.4 9.7 %copy-start.12 = (s32[128]{0:T(128)S(1)}, s32[128]{0:T(128)}, u32[]{:S(2)}) copy-start(s32[128]{0:T(128)} %param.27) | copy-start | bytes 1540
  42.4 9.8 %copy-start.9 = (s32[80]{0:T(128)S(1)}, s32[80]{0:T(128)}, u32[]{:S(2)}) copy-start(s32[80]{0:T(128)} %param.25) | copy-start | bytes 964
  42.4 9.8 %copy-start.10 = (s32[80]{0:T(128)S(1)}, s32[80]{0:T(128)}, u32[]{:S(2)}) copy-start(s32[80]{0:T(128)} %param.24) | copy-start | bytes 964
  42.4 10.0 %copy-start.11 = (s32[128]{0:T(128)S(1)}, s32[128]{0:T(128)}, u32[]{:S(2)}) copy-start(s32[128]{0:T(128)} %param.26) | copy-start | bytes 1540
  42.4 118.5 %all-to-all-start = ((bf16[8,128,2048]{2,1,0:T(8,128)(2,1)}), bf16[8,128,2048]{2,1,0:T(8,128)(2,1)}, u32[]{:S(2)}, u32[]{:S(2)}) async-start(bf16[8,128,2048]{2,1,0:T(8,128)(2,1)} %bitcast.85), calls=%async_computation | async-start | bytes 8388608 | tf_op jit(solution)/shard_map/all_to_all | solution.py:140
  50.8 137.6 %all-gather.7.cloned.1.call-start = ((), (), s32[]{:S(2)}) async-start(), calls=%async_computation.2 | async-start | bytes 4718592 | tf_op jit(solution)/shard_map/all_gather | solution.py:141
  51.8 267.7 %all-reduce.6.cloned.1.call-start = ((), (), s32[]{:S(2)}) async-start(), calls=%async_computation.3 | async-start | bytes 4194304 | tf_op jit(solution)/shard_map/psum | solution.py:162
  92.5 1.2 copy-start.13
  96.8 1.8 copy-start.4
  161.0 3.8 copy-start.8
  203.4 5.1 copy-start.3
  203.4 235.5 %all-reduce.8.cloned.1.call-start = ((), (), s32[]{:S(2)}) async-start(), calls=%async_computation.4 | async-start | bytes 3670016
  208.9 111.8 %copy-start.5 = (bf16[128,3584]{1,0:T(8,128)(2,1)S(1)}, bf16[128,3584]{1,0:T(8,128)(2,1)}, u32[]{:S(2)}) copy-start(bf16[128,3584]{1,0:T(8,128)(2,1)} %param.17) | copy-start | bytes 2752516
  211.6 110.7 %copy-start.14 = (u32[256]{0:T(256)S(1)}, u32[256]{0:T(256)}, u32[]{:S(2)}) copy-start(u32[256]{0:T(256)} %constant.96) | copy-start | bytes 3076
  211.7 228.4 %copy-start.7 = (bf16[4,3584]{1,0:T(4,128)(2,1)S(1)}, bf16[4,3584]{1,0:T(4,128)(2,1)}, u32[]{:S(2)}) copy-start(bf16[4,3584]{1,0:T(4,128)(2,1)} %param.14) | copy-start | bytes 86020
  322.3 265.7 %all-reduce.10.cloned.1.call-start = ((), (), s32[]{:S(2)}) async-start(), calls=%async_computation.5 | async-start | bytes 1835008
Sparse Core Ops, SparseCore 0:
  40.2 50.2 all-gather.4
  92.1 96.1 all-gather.6
  203.5 115.9 all-reduce.5
  322.7 116.2 all-reduce.7
  475.4 112.5 all-reduce.9
